TPU v7x, 256 devices: a whole 4x4x8 slice. The times are simulated.
256 devices in a mesh: win: 4 (over y_lo, core), tile: 64 (over x, y_hi, z).
Axes of the slice: x: 4, y: 4 (y_hi: 2, y_lo: 2; y = y_hi * 2 + y_lo), z: 8, core: 2. Of those that a mesh axis runs over, the one named last changes fastest.
Arguments:
- initial: float32 [4, 64, 36, 4096], P('win', 'tile'), may hold values from -6 to 6
- courant_x: bfloat16 [4, 64, 36, 4096], P('win', 'tile'), may hold values from 0.099609375 to 2.890625
- courant_y: bfloat16 [4, 64, 36, 4096], P('win', 'tile'), may hold values from 0.099609375 to 2.890625
- observed: float32 [4, 64, 64, 64], P('win', 'tile'), may hold values from -3 to 3
- precision_w: float32 [4, 64, 64, 64], P('win', 'tile'), may hold values from 0.2 to 2
- kernel: float32 [36], replicated, may hold values from 0.1 to 1
- profile: float32 [36], replicated, may hold values from 0.05 to 1
- emission: float32 [64, 64, 64], P('tile'), may hold values from -6 to 6
- edges: int32 [6, 64], replicated, may hold values from 0 to 63, as said below
Outputs:
- gradient: float32 [64, 64, 64], P('tile', 'win')
Inputs may be any that keep to these rules, and one draw needn't show every extreme that they name: edges[0, t] is (t - 1) or (t - 16) modulo 64, and edges[3, t] is (t - 2) or (t - 32) modulo 64; each of the four occurs for some tile; rows 1, 2, 4 and 5 hold 0 or 1, each value at some tile.
All inputs are finite; a program needn't handle non-finite values.
Results may differ from a plain program's by a relative error of at most 0.0003.
Values sent between devices are 32-bit elements; how exact they have to be, the bound alone decides.
A program may use at most 64 MiB of HBM per device.

v0:
```python
import jax
import jax.numpy as jnp
from jax import lax
from jax.sharding import PartitionSpec as P

STEPS = 2


def from_behind(block, axis, distance):
    devices = range(lax.axis_size(axis))
    route = [((i - distance) % len(devices), i) for i in devices]
    return lax.ppermute(block, axis, route)


def advect_along(tracer_field, rim_cells, courant, along):
    side_len = tracer_field.shape[along]
    extended = jnp.concatenate([rim_cells, tracer_field], along)
    edge_speed = lax.slice_in_dim(courant, side_len - 1, side_len, axis=along)
    inflow = jnp.zeros_like(tracer_field)
    outlet = jnp.zeros_like(edge_speed)
    for depth in range(1, 4):
        inflow = inflow + lax.slice_in_dim(
            extended, 3 - depth, 3 - depth + side_len, axis=along
        ) * jnp.clip(courant - (depth - 1), 0.0, 1.0)
        outlet = outlet + lax.slice_in_dim(
            tracer_field, side_len - depth, side_len - depth + 1, axis=along
        ) * jnp.clip(edge_speed - (depth - 1), 0.0, 1.0)
    outflow = jnp.concatenate([lax.slice_in_dim(inflow, 1, side_len, axis=along), outlet], along)
    return tracer_field - (outflow - inflow)


def advect_adjoint(sensitivity, courant, along):
    rim_shape = list(sensitivity.shape)
    rim_shape[along] = 3
    blank_field = jnp.zeros_like(sensitivity)
    blank_rim = jnp.zeros(tuple(rim_shape), jnp.float32)
    unused, pullback = jax.vjp(
        lambda tracer_field, rim_cells: advect_along(tracer_field, rim_cells, courant, along),
        blank_field,
        blank_rim,
    )
    return pullback(sensitivity)


def strips(tracer_field):
    side_len = tracer_field.shape[-1]
    east_strip = jnp.swapaxes(tracer_field[..., side_len - 3 :][..., ::-1], -1, -2)
    north_strip = tracer_field[..., side_len - 3 :, :][..., ::-1, :]
    return (east_strip, north_strip)


def add_strips(tracer_field_adjoint, east_bar, north_bar):
    side_len = tracer_field_adjoint.shape[-1]
    tracer_field_adjoint = tracer_field_adjoint.at[..., side_len - 3 :].add(
        jnp.swapaxes(east_bar, -1, -2)[..., ::-1]
    )
    return tracer_field_adjoint.at[..., side_len - 3 :, :].add(north_bar[..., ::-1, :])


def as_halo(panel, along):
    if along == 3:
        return jnp.swapaxes(panel[..., ::-1, :], -1, -2)
    return panel[..., ::-1, :]


def halo_back(rim_bar, along):
    if along == 3:
        return jnp.swapaxes(rim_bar, -1, -2)[..., ::-1, :]
    return rim_bar[..., ::-1, :]


def reverse_along(panel, flagged):
    return jnp.where(flagged, panel[..., ::-1], panel)


def own_entries(edges, position, base, tile_count, nearest):
    entries = lax.dynamic_slice_in_dim(edges, position, 1, 1)[:, 0]
    distant_indicator = entries[base] != (position - nearest) % tile_count
    return (distant_indicator, entries[base + 1], entries[base + 2])


def collect_receiver_index(tracer_field, local_details, shift_amounts, transfer_buffer):
    east_strip, north_strip = strips(tracer_field)
    stacked_panels = jnp.stack([east_strip, north_strip])
    received_neighbor = transfer_buffer(stacked_panels, shift_amounts[0])
    received_distant = transfer_buffer(stacked_panels, shift_amounts[1])
    distant_indicator, edge_code, flip_code = local_details
    arrived = jnp.where(distant_indicator, received_distant, received_neighbor)
    panel = jnp.where(edge_code == 0, arrived[0], arrived[1])
    return reverse_along(panel, flip_code == 1)


def backward_receiver_index(
    tracer_field_adjoint, panel_adjoint_value, local_details, shift_amounts, transfer_buffer
):
    distant_indicator, edge_code, flip_code = local_details
    returned = reverse_along(panel_adjoint_value, flip_code == 1)
    blank_panel = jnp.zeros_like(returned)
    stacked_panels = jnp.stack(
        [
            jnp.where(edge_code == 0, returned, blank_panel),
            jnp.where(edge_code == 0, blank_panel, returned),
        ]
    )
    empty_stacked_panels = jnp.zeros_like(stacked_panels)
    received_neighbor = transfer_buffer(
        jnp.where(distant_indicator, empty_stacked_panels, stacked_panels), -shift_amounts[0]
    )
    received_distant = transfer_buffer(
        jnp.where(distant_indicator, stacked_panels, empty_stacked_panels), -shift_amounts[1]
    )
    summed = received_neighbor + received_distant
    return add_strips(tracer_field_adjoint, summed[0], summed[1])


def body(initial, courant_x, courant_y, observed, precision_w, kernel, profile, emission, edges):
    side_len = observed.shape[-1]
    cube_shape = (initial.shape[0], initial.shape[2], side_len, side_len)
    tracer = initial[:, 0].reshape(cube_shape)
    speed_x = courant_x[:, 0].astype(jnp.float32).reshape(cube_shape)
    speed_y = courant_y[:, 0].astype(jnp.float32).reshape(cube_shape)
    source_rate = profile[None, :, None, None] * emission[0][None, None]
    tile_count = lax.axis_size("tile")
    position = lax.axis_index("tile")
    offsets_x = (1, tile_count // 4)
    offsets_y = (2, tile_count // 2)
    own_x = own_entries(edges, position, 0, tile_count, 1)
    own_y = own_entries(edges, position, 3, tile_count, 2)

    def carry_x(payload, offset):
        return from_behind(payload, "tile", offset)

    def carry_y(payload, offset):
        return from_behind(payload, "tile", offset)

    def return_x(payload, offset):
        return from_behind(payload, "tile", offset)

    def return_y(payload, offset):
        return from_behind(payload, "tile", offset)

    for step_index in range(STEPS):
        tracer = advect_along(
            tracer,
            as_halo(collect_receiver_index(tracer, own_x, offsets_x, carry_x), 3),
            speed_x,
            3,
        )
        tracer = advect_along(
            tracer,
            as_halo(collect_receiver_index(tracer, own_y, offsets_y, carry_y), 2),
            speed_y,
            2,
        )
        tracer = tracer + source_rate
    weight_sum = jnp.sum(kernel)
    column = jnp.sum(kernel[None, :, None, None] * tracer, axis=1) / weight_sum
    misfit = column - observed[:, 0]
    adjoint = (precision_w[:, 0] * misfit)[:, None] * (kernel[None, :, None, None] / weight_sum)
    gradient = jnp.zeros(emission.shape[1:], jnp.float32)
    for step_index in range(STEPS):
        gradient = gradient + jnp.sum(profile[None, :, None, None] * adjoint, axis=(0, 1))
        if step_index + 1 < STEPS:
            adjoint, rim_bar = advect_adjoint(adjoint, speed_y, 2)
            adjoint = backward_receiver_index(
                adjoint, halo_back(rim_bar, 2), own_y, offsets_y, return_y
            )
            adjoint, rim_bar = advect_adjoint(adjoint, speed_x, 3)
            adjoint = backward_receiver_index(
                adjoint, halo_back(rim_bar, 3), own_x, offsets_x, return_x
            )
    summed_all = lax.psum(gradient, "win")
    row_count = gradient.shape[0] // lax.axis_size("win")
    share_rows = lax.dynamic_slice_in_dim(
        summed_all, lax.axis_index("win") * row_count, row_count, 0
    )
    return share_rows[None]


def solution(mesh):
    placed = (
        P("win", "tile", None, None),
        P("win", "tile", None, None),
        P("win", "tile", None, None),
        P("win", "tile", None, None),
        P("win", "tile", None, None),
        P(),
        P(),
        P("tile", None, None),
        P(),
    )
    return jax.shard_map(
        body, mesh=mesh, in_specs=placed, out_specs=P("tile", "win", None), check_vma=False
    )
```

profile of v0, /device:TPU:1, one launch (start us, length us, event | category | flops | bytes accessed | tf_op | source)
XLA Modules:
  0.0 277.5 jit_solution(16219852052872074876)
XLA Ops:
  27.1 3.3 %rev.75 = f32[1,36,3,64]{2,1,3,0:T(8,128)} reverse(f32[1,36,3,64]{2,1,3,0:T(8,128)} %reverse_select_fusion.1), dimensions={2} | reverse | bytes 55296 | tf_op jit(solution)/shard_map/rev | solution.py:62
  30.5 5.5 %fusion.53 = (f32[1,36,64,64]{3,1,2,0:T(8,128)S(1)}, f32[1,36,64,64]{3,1,2,0:T(8,128)}) fusion(f32[1,36,64,64]{3,2,0,1:T(8,128)} %reshape.545, f32[1,36,64,64]{3,1,2,0:T(8,128)S(1)} %copy.200, f32[1,36,64,3]{3,1,2,0:T(8,128)} %bitcast.80), kind=kLoop, calls=%fused_computation.160 | loop fusion | flops 1916928 | bytes 2386944 | tf_op jit(solution)/shard_map/convert_element_type | solution.py:120
  40.8 2.8 %fusion.24 = f32[1,36,64,1]{3,1,2,0:T(8,128)S(1)} fusion(f32[1,36,64,1]{3,1,2,0:T(8,128)} %copy.199, f32[1,36,64,64]{3,1,2,0:T(8,128)S(1)} %copy.200, f32[1,36,64,64]{3,1,2,0:T(8,128)S(1)} %get-tuple-element.82), kind=kLoop, calls=%fused_computation.53 | loop fusion | flops 18432 | bytes 55296 | tf_op jit(solution)/shard_map/add | solution.py:25
  56.4 7.5 %collective-permute-done.3 = f32[2,1,36,3,64]{4,2,3,1,0:T(8,128)S(1)} collective-permute-done((f32[2,1,36,3,64]{4,2,3,1,0:T(8,128)S(1)}, f32[2,1,36,3,64]{4,2,3,1,0:T(8,128)S(1)}, u32[]{:S(2)}, u32[]{:S(2)}) %collective-permute-start.3) | collective-permute-done | bytes 55328 | tf_op jit(solution)/shard_map/ppermute | solution.py:12
  72.0 3.8 %fusion.17 = f32[1,36,64,1]{3,1,2,0:T(8,128)} fusion(f32[1,36,64,1]{3,1,2,0:T(8,128)} %copy.199, f32[1,36,64,64]{3,1,2,0:T(8,128)S(1)} %multiply_add_fusion.1, f32[1,36,64,64]{3,1,2,0:T(8,128)S(1)} %get-tuple-element.82), kind=kLoop, calls=%fused_computation.38 | loop fusion | flops 18432 | bytes 55296 | tf_op jit(solution)/shard_map/add | solution.py:25
  87.2 3.3 %rev.83 = f32[1,36,3,64]{2,1,3,0:T(8,128)} reverse(f32[1,36,3,64]{2,1,3,0:T(8,128)} %reverse_select_fusion), dimensions={2} | reverse | bytes 55296 | tf_op jit(solution)/shard_map/rev | solution.py:62
  90.5 4.4 %fusion.20 = f32[1,36,64,64]{3,1,2,0:T(8,128)S(1)} fusion(f32[1,36,64,64]{3,1,2,0:T(8,128)S(1)} %multiply_add_fusion.1, f32[1,36,64,3]{3,1,2,0:T(8,128)} %bitcast.79, f32[1,36,64,64]{3,2,0,1:T(8,128)} %reshape.545), kind=kLoop, calls=%fused_computation.44 | loop fusion | flops 1916928 | bytes 1797120 | tf_op jit(solution)/shard_map/add | solution.py:22
  101.5 4.0 %collective-permute-done.6 = f32[2,1,36,3,64]{4,2,3,1,0:T(8,128)S(1)} collective-permute-done((f32[2,1,36,3,64]{4,2,3,1,0:T(8,128)S(1)}, f32[2,1,36,3,64]{4,2,3,1,0:T(8,128)S(1)}, u32[]{:S(2)}, u32[]{:S(2)}) %collective-permute-start.6) | collective-permute-done | bytes 55328 | tf_op jit(solution)/shard_map/ppermute | solution.py:12
  105.5 5.7 %collective-permute-done.7 = f32[2,1,36,3,64]{4,2,3,1,0:T(8,128)S(1)} collective-permute-done((f32[2,1,36,3,64]{4,2,3,1,0:T(8,128)S(1)}, f32[2,1,36,3,64]{4,2,3,1,0:T(8,128)S(1)}, u32[]{:S(2)}, u32[]{:S(2)}) %collective-permute-start.7) | collective-permute-done | bytes 55328 | tf_op jit(solution)/shard_map/ppermute | solution.py:12
  111.4 3.3 %fusion.5 = (f32[1,36,64,64]{3,1,2,0:T(8,128)S(1)}, f32[1,36,64,64]{3,1,2,0:T(8,128)}) fusion(f32[1,36,64,64]{3,1,2,0:T(8,128)S(1)} %copy-done.5, f32[1,36,3,64]{3,1,2,0:T(8,128)S(1)} %rev.87, f32[1,36,64,64]{3,2,0,1:T(8,128)} %reshape.546), kind=kLoop, calls=%fused_computation.20 | loop fusion | flops 1916928 | bytes 2386944 | tf_op jit(solution)/shard_map/add | solution.py:22
  121.5 2.9 %copy.219 = f32[1,36,64,64]{2,1,3,0:T(8,128)} copy(f32[1,36,64,64]{3,1,2,0:T(8,128)} %get-tuple-element.79) | data formatting | bytes 1179648 | tf_op jit(solution)/shard_map/jit(clip)/min | solution.py:24
  126.0 3.6 %fusion.51 = (f32[1,36,64,64]{2,1,3,0:T(8,128)}, f32[1,36,64,64]{2,1,3,0:T(8,128)}) fusion(f32[1,36,64,64]{2,1,3,0:T(8,128)} %copy.219, f32[1,36,63,64]{2,1,3,0:T(8,128)} %copy.271, f32[36]{0:T(128)S(1)} %broadcast_divide_fusion, f32[64,64]{0,1:T(8,128)S(1)} %copy.212), kind=kLoop, calls=%fused_computation.158 | loop fusion | flops 442368 | bytes 2366608 | tf_op jit(solution)/shard_map/transpose(jvp())/mul | solution.py:22
  129.6 2.9 %copy.217 = f32[1,36,64,64]{3,1,2,0:T(8,128)} copy(f32[1,36,64,64]{2,1,3,0:T(8,128)} %get-tuple-element.56) | data formatting | bytes 1179648 | tf_op jit(solution)/shard_map/transpose(jvp())/add_any | solution.py:28
  140.1 2.6 rev.88
  142.7 2.6 rev.89
  145.3 2.9 %copy.250 = f32[1,36,64,64]{3,1,2,0:T(8,128)} copy(f32[1,36,64,64]{2,1,3,0:T(8,128)} %split.34) | data formatting | bytes 1179648
  149.7 2.7 pad_maximum_fusion
  156.9 2.6 copy.225
  166.7 17.9 %scatter-add.14 = f32[1,36,64,64]{3,1,2,0:T(8,128)S(1)} dynamic-update-slice(f32[1,36,64,64]{3,1,2,0:T(8,128)S(1)} %add_add_fusion, f32[1,36,64,3]{3,1,2,0:T(8,128)} %copy.231, s32[]{:T(128)} %constant.141.clone.1, s32[]{:T(128)} %constant.141.clone.1, s32[]{:T(128)} %constant.141.clone.1, s32[]{:T(128)} %constant.153.clone.1) | dynamic-update-slice | bytes 55300 | tf_op jit(solution)/shard_map/scatter-add | solution.py:54
  187.5 4.1 %fusion.40 = (f32[1,36,64,1]{3,1,2,0:T(8,128)}, f32[1,36,64,1]{3,1,2,0:T(8,128)}, f32[1,36,64,1]{3,1,2,0:T(8,128)}) fusion(f32[1,36,64,64]{3,1,2,0:T(8,128)S(1)} %get-tuple-element.82, f32[1,36,64,64]{3,1,2,0:T(8,128)} %neg.17), kind=kLoop, calls=%fused_computation.103 | loop fusion | flops 11520 | bytes 46080 | tf_op jit(solution)/shard_map/transpose(jvp())/mul | solution.py:25
  195.0 2.6 rev.92
  197.6 2.6 rev.93
  206.2 2.7 fusion
  211.4 3.5 %collective-permute-start.10 = (f32[2,1,36,3,64]{4,0,3,2,1:T(2,128)S(1)}, f32[2,1,36,3,64]{4,0,3,2,1:T(2,128)S(1)}, u32[]{:S(2)}, u32[]{:S(2)}) collective-permute-start(f32[2,1,36,3,64]{4,0,3,2,1:T(2,128)S(1)} %copy.238), channel_id=1, source_target_pairs={{1,0},{2,1},{3,2},{4,3},{5,4},{6,5},{7,6},{8,7},{9,8},{10,9},{11,1... | collective-permute-start | bytes 165896 | tf_op jit(solution)/shard_map/ppermute | solution.py:12
  214.9 2.6 copy.239
  225.5 2.8 %add.201 = f32[2,1,36,3,64]{3,2,4,1,0:T(8,128)S(1)} add(f32[2,1,36,3,64]{3,2,4,1,0:T(8,128)} %copy.240, f32[2,1,36,3,64]{3,2,4,1,0:T(8,128)} %copy.241) | non-fusion elementwise | flops 13824 | bytes 165888 | tf_op jit(solution)/shard_map/add | solution.py:112
  229.6 3.3 %rev.94 = f32[1,36,64,3]{3,1,2,0:T(8,128)} reverse(f32[1,36,64,3]{3,1,2,0:T(8,128)} %get-tuple-element.61), dimensions={3} | reverse | bytes 55296 | tf_op jit(solution)/shard_map/rev | solution.py:55
  232.9 2.9 %add.202 = f32[1,36,64,3]{3,1,2,0:T(8,128)} add(f32[1,36,64,3]{3,1,2,0:T(8,128)} %copy.252, f32[1,36,64,3]{3,1,2,0:T(8,128)} %rev.94) | non-fusion elementwise | flops 6912 | bytes 82944 | tf_op jit(solution)/shard_map/add | solution.py:54
  237.6 2.6 rev.95
  240.2 2.8 %slice_add_fusion = f32[1,36,3,64]{2,1,3,0:T(8,128)} fusion(f32[1,36,3,64]{2,1,3,0:T(8,128)} %rev.95, f32[1,36,64,64]{2,1,3,0:T(8,128)S(1)} %constant_dynamic-update-slice_fusion), kind=kLoop, calls=%fused_computation.32 | loop fusion | flops 6912 | bytes 82944 | tf_op jit(solution)/shard_map/add | solution.py:57
  243.0 18.0 %scatter-add.19 = f32[1,36,64,64]{2,1,3,0:T(8,128)S(1)} dynamic-update-slice(f32[1,36,64,64]{2,1,3,0:T(8,128)S(1)} %constant_dynamic-update-slice_fusion, f32[1,36,3,64]{2,1,3,0:T(8,128)} %slice_add_fusion, s32[]{:T(128)} %constant.141.clone.1, s32[]{:T(128)} %constant.141.clone.1, s32[]{:T(128)} %constant.153.clone.1, s32[]{:T(128)} %constant.141.clone.1) | dynamic-update-slice | bytes 55300 | tf_op jit(solution)/shard_map/scatter-add | solution.py:57
  261.6 15.0 %psum.7 = f32[64,64]{0,1:T(8,128)S(1)} all-reduce(f32[64,64]{0,1:T(8,128)S(1)} %add.204), channel_id=1, replica_groups=mesh['win'=4,'tile'=64] {'win'}, use_global_device_ids=true, to_apply=%region_4.5 | all-reduce | flops 4096 | bytes 32768 | tf_op jit(solution)/shard_map/psum | solution.py:172
  (198 shorter events, 122.9 us)
Async XLA Ops:
  0.0 11.2 %copy-start = (s32[6,64]{1,0:T(8,128)S(1)}, s32[6,64]{1,0:T(8,128)}, u32[]{:S(2)}) copy-start(s32[6,64]{1,0:T(8,128)} %param.25) | copy-start | bytes 4612
  3.0 8.9 %copy-start.6 = (f32[1,36,64,64]{3,2,0,1:T(8,128)}, f32[1,36,64,64]{3,2,0,1:T(8,128)S(1)}, u32[]{:S(2)}) copy-start(f32[1,36,64,64]{3,2,0,1:T(8,128)S(1)} %reshape_squeeze.3) | copy-start | bytes 1769476
  7.3 5.3 %copy-start.22 = (bf16[1,1,36,4096]{3,2,1,0:T(8,128)(2,1)S(1)}, bf16[1,1,36,4096]{3,2,1,0:T(8,128)(2,1)}, u32[]{:S(2)}) copy-start(bf16[1,1,36,4096]{3,2,1,0:T(8,128)(2,1)} %param.18) | copy-start | bytes 884740
  7.3 9.4 %collective-permute-start = (f32[2,1,36,3,64]{4,0,3,2,1:T(2,128)S(1)}, f32[2,1,36,3,64]{4,0,3,2,1:T(2,128)S(1)}, u32[]{:S(2)}, u32[]{:S(2)}) collective-permute-start(f32[2,1,36,3,64]{4,0,3,2,1:T(2,128)S(1)} %pad_maximum_fusion.9), channel_id=1, source_target_pairs={{48,0},{49,1},{50,2},{51,3},{52,4},{53,5},{54,6},{55,7},{56,8},{57... | collective-permute-start | bytes 165896 | tf_op jit(solution)/shard_map/ppermute | solution.py:12
  9.4 12.0 %collective-permute-start.1 = (f32[2,1,36,3,64]{4,0,3,2,1:T(2,128)S(1)}, f32[2,1,36,3,64]{4,0,3,2,1:T(2,128)S(1)}, u32[]{:S(2)}, u32[]{:S(2)}) collective-permute-start(f32[2,1,36,3,64]{4,0,3,2,1:T(2,128)S(1)} %pad_maximum_fusion.9), channel_id=1, source_target_pairs={{63,0},{0,1},{1,2},{2,3},{3,4},{4,5},{5,6},{6,7},{7,8},{8,9},{9,10... | collective-permute-start | bytes 165896 | tf_op jit(solution)/shard_map/ppermute | solution.py:12
  12.6 3.5 %copy-start.28 = (f32[36]{0:T(128)S(1)}, f32[36]{0:T(128)}, u32[]{:S(2)}) copy-start(f32[36]{0:T(128)} %param.22) | copy-start | bytes 436
  40.7 2.8 %copy-start.11 = (f32[1,36,64,64]{3,1,2,0:T(8,128)S(1)}, f32[1,36,64,64]{3,1,2,0:T(8,128)}, u32[]{:S(2)}) copy-start(f32[1,36,64,64]{3,1,2,0:T(8,128)} %get-tuple-element.83) | copy-start | bytes 1769476
  45.8 20.6 %copy-start.2 = (f32[1,36,64,64]{3,1,2,0:T(8,128)}, f32[1,36,64,64]{3,1,2,0:T(8,128)S(1)}, u32[]{:S(2)}) copy-start(f32[1,36,64,64]{3,1,2,0:T(8,128)S(1)} %fusion.30) | copy-start | bytes 1769476
  47.3 5.9 %copy-start.23 = (bf16[1,1,36,4096]{3,2,1,0:T(8,128)(2,1)S(1)}, bf16[1,1,36,4096]{3,2,1,0:T(8,128)(2,1)}, u32[]{:S(2)}) copy-start(bf16[1,1,36,4096]{3,2,1,0:T(8,128)(2,1)} %param.19) | copy-start | bytes 884740
  49.1 7.3 %collective-permute-start.2 = (f32[2,1,36,3,64]{4,2,3,1,0:T(8,128)S(1)}, f32[2,1,36,3,64]{4,2,3,1,0:T(8,128)S(1)}, u32[]{:S(2)}, u32[]{:S(2)}) collective-permute-start(f32[2,1,36,3,64]{4,2,3,1,0:T(8,128)S(1)} %pad_maximum_fusion.6), channel_id=1, source_target_pairs={{32,0},{33,1},{34,2},{35,3},{36,4},{37,5},{38,6},{39,7},{40,8},{41... | collective-permute-start | bytes 165896 | tf_op jit(solution)/shard_map/ppermute | solution.py:12
  50.7 13.2 %collective-permute-start.3 = (f32[2,1,36,3,64]{4,2,3,1,0:T(8,128)S(1)}, f32[2,1,36,3,64]{4,2,3,1,0:T(8,128)S(1)}, u32[]{:S(2)}, u32[]{:S(2)}) collective-permute-start(f32[2,1,36,3,64]{4,2,3,1,0:T(8,128)S(1)} %pad_maximum_fusion.6), channel_id=1, source_target_pairs={{62,0},{63,1},{0,2},{1,3},{2,4},{3,5},{4,6},{5,7},{6,8},{7,9},{8,1... | collective-permute-start | bytes 165896 | tf_op jit(solution)/shard_map/ppermute | solution.py:12
  66.4 1.8 copy-start.3
  66.4 1.8 copy-start.24
  71.8 5.0 %collective-permute-start.4 = (f32[2,1,36,3,64]{4,2,3,1,0:T(8,128)S(1)}, f32[2,1,36,3,64]{4,2,3,1,0:T(8,128)S(1)}, u32[]{:S(2)}, u32[]{:S(2)}) collective-permute-start(f32[2,1,36,3,64]{4,2,3,1,0:T(8,128)S(1)} %pad_maximum_fusion.7), channel_id=1, source_target_pairs={{48,0},{49,1},{50,2},{51,3},{52,4},{53,5},{54,6},{55,7},{56,8},{57... | collective-permute-start | bytes 165896 | tf_op jit(solution)/shard_map/ppermute | solution.py:12
  71.9 9.5 %collective-permute-start.5 = (f32[2,1,36,3,64]{4,2,3,1,0:T(8,128)S(1)}, f32[2,1,36,3,64]{4,2,3,1,0:T(8,128)S(1)}, u32[]{:S(2)}, u32[]{:S(2)}) collective-permute-start(f32[2,1,36,3,64]{4,2,3,1,0:T(8,128)S(1)} %pad_maximum_fusion.7), channel_id=1, source_target_pairs={{63,0},{0,1},{1,2},{2,3},{3,4},{4,5},{5,6},{6,7},{7,8},{8,9},{9,10... | collective-permute-start | bytes 165896 | tf_op jit(solution)/shard_map/ppermute | solution.py:12
  98.3 2.5 copy-start.5
  100.2 5.3 %collective-permute-start.6 = (f32[2,1,36,3,64]{4,2,3,1,0:T(8,128)S(1)}, f32[2,1,36,3,64]{4,2,3,1,0:T(8,128)S(1)}, u32[]{:S(2)}, u32[]{:S(2)}) collective-permute-start(f32[2,1,36,3,64]{4,2,3,1,0:T(8,128)S(1)} %pad_maximum_fusion.8), channel_id=1, source_target_pairs={{32,0},{33,1},{34,2},{35,3},{36,4},{37,5},{38,6},{39,7},{40,8},{41... | collective-permute-start | bytes 165896 | tf_op jit(solution)/shard_map/ppermute | solution.py:12
  100.3 10.9 %collective-permute-start.7 = (f32[2,1,36,3,64]{4,2,3,1,0:T(8,128)S(1)}, f32[2,1,36,3,64]{4,2,3,1,0:T(8,128)S(1)}, u32[]{:S(2)}, u32[]{:S(2)}) collective-permute-start(f32[2,1,36,3,64]{4,2,3,1,0:T(8,128)S(1)} %pad_maximum_fusion.8), channel_id=1, source_target_pairs={{62,0},{63,1},{0,2},{1,3},{2,4},{3,5},{4,6},{5,7},{6,8},{7,9},{8,1... | collective-permute-start | bytes 165896 | tf_op jit(solution)/shard_map/ppermute | solution.py:12
  121.5 2.9 %slice-start = ((f32[1,36,64,64]{3,1,2,0:T(8,128)}), f32[1,36,63,64]{3,1,2,0:T(8,128)S(1)}, s32[]{:S(2)}) async-start(f32[1,36,64,64]{3,1,2,0:T(8,128)} %copy-done.14), calls=%async_computation | async-start | bytes 2580480 | tf_op jit(solution)/shard_map/transpose(jvp())/split | solution.py:28
  129.6 2.9 %copy-start.8 = (f32[1,36,64,64]{3,2,0,1:T(8,128)S(1)}, f32[1,36,64,64]{3,2,0,1:T(8,128)}, u32[]{:S(2)}) copy-start(f32[1,36,64,64]{3,2,0,1:T(8,128)} %reshape.546) | copy-start | bytes 1769476
  145.3 3.0 %copy-start.18 = (f32[1,36,3,64]{2,1,3,0:T(8,128)S(1)}, f32[1,36,3,64]{2,1,3,0:T(8,128)}, u32[]{:S(2)}) copy-start(f32[1,36,3,64]{2,1,3,0:T(8,128)} %rev.88) | copy-start | bytes 82948
  154.9 10.2 %collective-permute-start.9 = (f32[2,1,36,3,64]{4,0,3,2,1:T(2,128)S(1)}, f32[2,1,36,3,64]{4,0,3,2,1:T(2,128)S(1)}, u32[]{:S(2)}, u32[]{:S(2)}) collective-permute-start(f32[2,1,36,3,64]{4,0,3,2,1:T(2,128)S(1)} %copy.228), channel_id=1, source_target_pairs={{32,0},{33,1},{34,2},{35,3},{36,4},{37,5},{38,6},{39,7},{40,8},{41... | collective-permute-start | bytes 165896 | tf_op jit(solution)/shard_map/ppermute | solution.py:12
  159.6 5.5 %collective-permute-start.8 = (f32[2,1,36,3,64]{4,0,3,2,1:T(2,128)S(1)}, f32[2,1,36,3,64]{4,0,3,2,1:T(2,128)S(1)}, u32[]{:S(2)}, u32[]{:S(2)}) collective-permute-start(f32[2,1,36,3,64]{4,0,3,2,1:T(2,128)S(1)} %copy.226), channel_id=1, source_target_pairs={{2,0},{3,1},{4,2},{5,3},{6,4},{7,5},{8,6},{9,7},{10,8},{11,9},{12,... | collective-permute-start | bytes 165896 | tf_op jit(solution)/shard_map/ppermute | solution.py:12
  187.5 4.1 %copy-start.9 = (f32[1,36,64,64]{3,2,0,1:T(8,128)S(1)}, f32[1,36,64,64]{3,2,0,1:T(8,128)}, u32[]{:S(2)}) copy-start(f32[1,36,64,64]{3,2,0,1:T(8,128)} %reshape.545) | copy-start | bytes 1769476
  187.5 4.1 %copy-start.12 = (f32[1,36,64,64]{3,1,2,0:T(8,128)S(1)}, f32[1,36,64,64]{3,1,2,0:T(8,128)}, u32[]{:S(2)}) copy-start(f32[1,36,64,64]{3,1,2,0:T(8,128)} %neg.17) | copy-start | bytes 1769476
  197.6 2.6 copy-start.15
  202.3 3.7 %copy-start.16 = (f32[1,36,3,64]{2,1,3,0:T(8,128)S(1)}, f32[1,36,3,64]{2,1,3,0:T(8,128)}, u32[]{:S(2)}) copy-start(f32[1,36,3,64]{2,1,3,0:T(8,128)} %rev.92) | copy-start | bytes 82948
  202.3 3.7 %copy-start.17 = (f32[1,36,3,64]{2,1,3,0:T(8,128)S(1)}, f32[1,36,3,64]{2,1,3,0:T(8,128)}, u32[]{:S(2)}) copy-start(f32[1,36,3,64]{2,1,3,0:T(8,128)} %rev.93) | copy-start | bytes 82948
  211.4 9.4 %collective-permute-start.10 = (f32[2,1,36,3,64]{4,0,3,2,1:T(2,128)S(1)}, f32[2,1,36,3,64]{4,0,3,2,1:T(2,128)S(1)}, u32[]{:S(2)}, u32[]{:S(2)}) collective-permute-start(f32[2,1,36,3,64]{4,0,3,2,1:T(2,128)S(1)} %copy.238), channel_id=1, source_target_pairs={{1,0},{2,1},{3,2},{4,3},{5,4},{6,5},{7,6},{8,7},{9,8},{10,9},{11,1... | collective-permute-start | bytes 165896 | tf_op jit(solution)/shard_map/ppermute | solution.py:12
  214.9 2.9 %copy-start.13 = (f32[1,36,64,64]{2,1,3,0:T(8,128)S(1)}, f32[1,36,64,64]{2,1,3,0:T(8,128)}, u32[]{:S(2)}) copy-start(f32[1,36,64,64]{2,1,3,0:T(8,128)} %copy.233) | copy-start | bytes 1769476
  217.5 5.7 %collective-permute-start.11 = (f32[2,1,36,3,64]{4,0,3,2,1:T(2,128)S(1)}, f32[2,1,36,3,64]{4,0,3,2,1:T(2,128)S(1)}, u32[]{:S(2)}, u32[]{:S(2)}) collective-permute-start(f32[2,1,36,3,64]{4,0,3,2,1:T(2,128)S(1)} %copy.239), channel_id=1, source_target_pairs={{16,0},{17,1},{18,2},{19,3},{20,4},{21,5},{22,6},{23,7},{24,8},{25... | collective-permute-start | bytes 165896 | tf_op jit(solution)/shard_map/ppermute | solution.py:12
  243.0 34.3 %copy-start.1 = (s32[6,64]{1,0:T(8,128)S(1)}, s32[6,64]{1,0:T(8,128)}, u32[]{:S(2)}) copy-start(s32[6,64]{1,0:T(8,128)} %param.25) | copy-start | bytes 4612
  (10 other events, 12.2 us)
where the time goes:
time: 283 us; the launch traced here: 278 us
  local copies, waits for them, and re-layouts  146 us (52%)
  other arithmetic  74.5 us (26%)
  waiting for transfers between devices  22.9 us (8%)
  blocking collectives  15 us (5%)
  starting transfers between devices  14.1 us (5%)
  between operations  4.68 us (2%)
    ppermute x12, waiting for transfers between devices, from_behind(): return lax.ppermute(block, axis, route)  22.9 us
    unnamed x67, local copies, waits for them, and re-layouts  20.8 us
    scatter-add x2, local copies, waits for them, and re-layouts, add_strips(): tracer_field_adjoint.at[..., side_len - 3:, :].add(north_bar[..., ::-1, :])  19.5 us
    scatter-add x2, local copies, waits for them, and re-layouts, add_strips(): tracer_field_adjoint.at[..., side_len - 3:]  17.9 us
    psum x1, blocking collectives, body(): summed_all = lax.psum(gradient, 'win')  15 us
    ppermute x6, local copies, waits for them, and re-layouts, from_behind(): return lax.ppermute(block, axis, route)  14.1 us
    ppermute x12, starting transfers between devices, from_behind(): return lax.ppermute(block, axis, route)  14.1 us
    add x2, other arithmetic, advect_along(): inflow + lax.slice_in_dim(extended, 3 - depth, 3 - depth + side_len, axis...  7.73 us
  transfers between devices with their start and end apart: 12, of which 6 were waited for; matrix products, arithmetic and copies ran while one was open for 11% of the time, Pallas kernels for 0%

commit v1 on v0

--- a/solution.py
+++ b/solution.py
@@ -4,6 +4,12 @@
 from jax.sharding import PartitionSpec as P
 
 STEPS = 2
+
+
+def gather_and_add(shard, axis):
+    parts = lax.all_gather(shard, axis, axis=0, tiled=False)
+    acc = parts.sum(axis=0)
+    return acc
 
 
 def from_behind(block, axis, distance):
@@ -169,7 +175,7 @@
             adjoint = backward_receiver_index(
                 adjoint, halo_back(rim_bar, 3), own_x, offsets_x, return_x
             )
-    summed_all = lax.psum(gradient, "win")
+    summed_all = gather_and_add(gradient, "win")
     row_count = gradient.shape[0] // lax.axis_size("win")
     share_rows = lax.dynamic_slice_in_dim(
         summed_all, lax.axis_index("win") * row_count, row_count, 0

time: 283 us -> 279 us (0.986)
  blocking collectives: 15 us -> 10.7 us
    psum x1 -> x0, blocking collectives: 15 us -> none  [body(): summed_all = lax.psum(gradient, 'win')]
    all_gather x0 -> x1, blocking collectives: none -> 10.7 us  [gather_and_add(): parts = lax.all_gather(shard, axis, axis=0, tiled=False)]
where the time goes in v1:
time: 279 us; the launch traced here: 273 us
  local copies, waits for them, and re-layouts  146 us (52%)
  other arithmetic  74.6 us (27%)
  waiting for transfers between devices  22.9 us (8%)
  starting transfers between devices  14.1 us (5%)
  blocking collectives  10.7 us (4%)
  between operations  4.68 us (2%)
    ppermute x12, waiting for transfers between devices, from_behind(): return lax.ppermute(block, axis, route)  22.9 us
    unnamed x67, local copies, waits for them, and re-layouts  20.8 us
    scatter-add x2, local copies, waits for them, and re-layouts, add_strips(): tracer_field_adjoint.at[..., side_len - 3:, :].add(north_bar[..., ::-1, :])  19.5 us
    scatter-add x2, local copies, waits for them, and re-layouts, add_strips(): tracer_field_adjoint.at[..., side_len - 3:]  17.9 us
    ppermute x6, local copies, waits for them, and re-layouts, from_behind(): return lax.ppermute(block, axis, route)  14.1 us
    ppermute x12, starting transfers between devices, from_behind(): return lax.ppermute(block, axis, route)  14.1 us
    all_gather x1, blocking collectives, gather_and_add(): parts = lax.all_gather(shard, axis, axis=0, tiled=False)  10.7 us
    add x2, other arithmetic, advect_along(): inflow + lax.slice_in_dim(extended, 3 - depth, 3 - depth + side_len, axis...  7.73 us
  transfers between devices with their start and end apart: 12, of which 6 were waited for; matrix products, arithmetic and copies ran while one was open for 11% of the time, Pallas kernels for 0%

profile of v1, /device:TPU:1, one launch (start us, length us, event | category | flops | bytes accessed | tf_op | source)
XLA Modules:
  0.0 273.3 jit_solution(8202946030276359137)
XLA Ops:
  27.1 3.3 %rev.75 = f32[1,36,3,64]{2,1,3,0:T(8,128)} reverse(f32[1,36,3,64]{2,1,3,0:T(8,128)} %reverse_select_fusion.1), dimensions={2} | reverse | bytes 55296 | tf_op jit(solution)/shard_map/rev | solution.py:68
  30.5 5.5 %fusion.53 = (f32[1,36,64,64]{3,1,2,0:T(8,128)S(1)}, f32[1,36,64,64]{3,1,2,0:T(8,128)}) fusion(f32[1,36,64,64]{3,2,0,1:T(8,128)} %reshape.557, f32[1,36,64,64]{3,1,2,0:T(8,128)S(1)} %copy.222, f32[1,36,64,3]{3,1,2,0:T(8,128)} %bitcast.82), kind=kLoop, calls=%fused_computation.160 | loop fusion | flops 1916928 | bytes 2386944 | tf_op jit(solution)/shard_map/convert_element_type | solution.py:126
  40.8 2.8 %fusion.24 = f32[1,36,64,1]{3,1,2,0:T(8,128)S(1)} fusion(f32[1,36,64,1]{3,1,2,0:T(8,128)} %copy.221, f32[1,36,64,64]{3,1,2,0:T(8,128)S(1)} %copy.222, f32[1,36,64,64]{3,1,2,0:T(8,128)S(1)} %get-tuple-element.82), kind=kLoop, calls=%fused_computation.53 | loop fusion | flops 18432 | bytes 55296 | tf_op jit(solution)/shard_map/add | solution.py:31
  56.4 7.5 %collective-permute-done.3 = f32[2,1,36,3,64]{4,2,3,1,0:T(8,128)S(1)} collective-permute-done((f32[2,1,36,3,64]{4,2,3,1,0:T(8,128)S(1)}, f32[2,1,36,3,64]{4,2,3,1,0:T(8,128)S(1)}, u32[]{:S(2)}, u32[]{:S(2)}) %collective-permute-start.3) | collective-permute-done | bytes 55328 | tf_op jit(solution)/shard_map/ppermute | solution.py:18
  72.0 3.8 %fusion.17 = f32[1,36,64,1]{3,1,2,0:T(8,128)} fusion(f32[1,36,64,1]{3,1,2,0:T(8,128)} %copy.221, f32[1,36,64,64]{3,1,2,0:T(8,128)S(1)} %multiply_add_fusion.1, f32[1,36,64,64]{3,1,2,0:T(8,128)S(1)} %get-tuple-element.82), kind=kLoop, calls=%fused_computation.38 | loop fusion | flops 18432 | bytes 55296 | tf_op jit(solution)/shard_map/add | solution.py:31
  87.2 3.3 %rev.83 = f32[1,36,3,64]{2,1,3,0:T(8,128)} reverse(f32[1,36,3,64]{2,1,3,0:T(8,128)} %reverse_select_fusion), dimensions={2} | reverse | bytes 55296 | tf_op jit(solution)/shard_map/rev | solution.py:68
  90.5 4.4 %fusion.20 = f32[1,36,64,64]{3,1,2,0:T(8,128)S(1)} fusion(f32[1,36,64,64]{3,1,2,0:T(8,128)S(1)} %multiply_add_fusion.1, f32[1,36,64,3]{3,1,2,0:T(8,128)} %bitcast.81, f32[1,36,64,64]{3,2,0,1:T(8,128)} %reshape.557), kind=kLoop, calls=%fused_computation.44 | loop fusion | flops 1916928 | bytes 1797120 | tf_op jit(solution)/shard_map/add | solution.py:28
  101.5 4.0 %collective-permute-done.6 = f32[2,1,36,3,64]{4,2,3,1,0:T(8,128)S(1)} collective-permute-done((f32[2,1,36,3,64]{4,2,3,1,0:T(8,128)S(1)}, f32[2,1,36,3,64]{4,2,3,1,0:T(8,128)S(1)}, u32[]{:S(2)}, u32[]{:S(2)}) %collective-permute-start.6) | collective-permute-done | bytes 55328 | tf_op jit(solution)/shard_map/ppermute | solution.py:18
  105.5 5.7 %collective-permute-done.7 = f32[2,1,36,3,64]{4,2,3,1,0:T(8,128)S(1)} collective-permute-done((f32[2,1,36,3,64]{4,2,3,1,0:T(8,128)S(1)}, f32[2,1,36,3,64]{4,2,3,1,0:T(8,128)S(1)}, u32[]{:S(2)}, u32[]{:S(2)}) %collective-permute-start.7) | collective-permute-done | bytes 55328 | tf_op jit(solution)/shard_map/ppermute | solution.py:18
  111.4 3.3 %fusion.5 = (f32[1,36,64,64]{3,1,2,0:T(8,128)S(1)}, f32[1,36,64,64]{3,1,2,0:T(8,128)}) fusion(f32[1,36,64,64]{3,1,2,0:T(8,128)S(1)} %copy-done.5, f32[1,36,3,64]{3,1,2,0:T(8,128)S(1)} %rev.87, f32[1,36,64,64]{3,2,0,1:T(8,128)} %reshape.558), kind=kLoop, calls=%fused_computation.20 | loop fusion | flops 1916928 | bytes 2386944 | tf_op jit(solution)/shard_map/add | solution.py:28
  121.5 2.9 %copy.241 = f32[1,36,64,64]{2,1,3,0:T(8,128)} copy(f32[1,36,64,64]{3,1,2,0:T(8,128)} %get-tuple-element.79) | data formatting | bytes 1179648 | tf_op jit(solution)/shard_map/jit(clip)/min | solution.py:30
  126.0 3.6 %fusion.51 = (f32[1,36,64,64]{2,1,3,0:T(8,128)}, f32[1,36,64,64]{2,1,3,0:T(8,128)}) fusion(f32[1,36,64,64]{2,1,3,0:T(8,128)} %copy.241, f32[1,36,63,64]{2,1,3,0:T(8,128)} %copy.298, f32[36]{0:T(128)S(1)} %broadcast_divide_fusion, f32[64,64]{0,1:T(8,128)S(1)} %copy.234), kind=kLoop, calls=%fused_computation.158 | loop fusion | flops 442368 | bytes 2366608 | tf_op jit(solution)/shard_map/transpose(jvp())/mul | solution.py:28
  129.6 2.9 %copy.239 = f32[1,36,64,64]{3,1,2,0:T(8,128)} copy(f32[1,36,64,64]{2,1,3,0:T(8,128)} %get-tuple-element.56) | data formatting | bytes 1179648 | tf_op jit(solution)/shard_map/transpose(jvp())/add_any | solution.py:34
  140.1 2.6 rev.88
  142.7 2.6 rev.89
  145.3 2.9 %copy.275 = f32[1,36,64,64]{3,1,2,0:T(8,128)} copy(f32[1,36,64,64]{2,1,3,0:T(8,128)} %split.34) | data formatting | bytes 1179648
  149.7 2.7 pad_maximum_fusion
  156.9 2.6 copy.247
  166.7 17.9 %scatter-add.14 = f32[1,36,64,64]{3,1,2,0:T(8,128)S(1)} dynamic-update-slice(f32[1,36,64,64]{3,1,2,0:T(8,128)S(1)} %add_add_fusion, f32[1,36,64,3]{3,1,2,0:T(8,128)} %copy.253, s32[]{:T(128)} %constant.141.clone.1, s32[]{:T(128)} %constant.141.clone.1, s32[]{:T(128)} %constant.141.clone.1, s32[]{:T(128)} %constant.153.clone.1) | dynamic-update-slice | bytes 55300 | tf_op jit(solution)/shard_map/scatter-add | solution.py:60
  187.5 4.1 %fusion.40 = (f32[1,36,64,1]{3,1,2,0:T(8,128)}, f32[1,36,64,1]{3,1,2,0:T(8,128)}, f32[1,36,64,1]{3,1,2,0:T(8,128)}) fusion(f32[1,36,64,64]{3,1,2,0:T(8,128)S(1)} %get-tuple-element.82, f32[1,36,64,64]{3,1,2,0:T(8,128)} %neg.17), kind=kLoop, calls=%fused_computation.103 | loop fusion | flops 11520 | bytes 46080 | tf_op jit(solution)/shard_map/transpose(jvp())/mul | solution.py:31
  195.0 2.6 rev.92
  197.6 2.6 rev.93
  206.2 2.7 fusion
  211.4 3.5 %collective-permute-start.10 = (f32[2,1,36,3,64]{4,0,3,2,1:T(2,128)S(1)}, f32[2,1,36,3,64]{4,0,3,2,1:T(2,128)S(1)}, u32[]{:S(2)}, u32[]{:S(2)}) collective-permute-start(f32[2,1,36,3,64]{4,0,3,2,1:T(2,128)S(1)} %copy.260), channel_id=1, source_target_pairs={{1,0},{2,1},{3,2},{4,3},{5,4},{6,5},{7,6},{8,7},{9,8},{10,9},{11,1... | collective-permute-start | bytes 165896 | tf_op jit(solution)/shard_map/ppermute | solution.py:18
  214.9 2.6 copy.261
  225.5 2.8 %add.209 = f32[2,1,36,3,64]{3,2,4,1,0:T(8,128)S(1)} add(f32[2,1,36,3,64]{3,2,4,1,0:T(8,128)} %copy.262, f32[2,1,36,3,64]{3,2,4,1,0:T(8,128)} %copy.263) | non-fusion elementwise | flops 13824 | bytes 165888 | tf_op jit(solution)/shard_map/add | solution.py:118
  229.6 3.3 %rev.94 = f32[1,36,64,3]{3,1,2,0:T(8,128)} reverse(f32[1,36,64,3]{3,1,2,0:T(8,128)} %get-tuple-element.61), dimensions={3} | reverse | bytes 55296 | tf_op jit(solution)/shard_map/rev | solution.py:61
  232.9 2.9 %add.210 = f32[1,36,64,3]{3,1,2,0:T(8,128)} add(f32[1,36,64,3]{3,1,2,0:T(8,128)} %copy.277, f32[1,36,64,3]{3,1,2,0:T(8,128)} %rev.94) | non-fusion elementwise | flops 6912 | bytes 82944 | tf_op jit(solution)/shard_map/add | solution.py:60
  237.6 2.6 rev.95
  240.2 2.8 %slice_add_fusion = f32[1,36,3,64]{2,1,3,0:T(8,128)} fusion(f32[1,36,3,64]{2,1,3,0:T(8,128)} %rev.95, f32[1,36,64,64]{2,1,3,0:T(8,128)S(1)} %constant_dynamic-update-slice_fusion), kind=kLoop, calls=%fused_computation.32 | loop fusion | flops 6912 | bytes 82944 | tf_op jit(solution)/shard_map/add | solution.py:63
  243.0 18.0 %scatter-add.19 = f32[1,36,64,64]{2,1,3,0:T(8,128)S(1)} dynamic-update-slice(f32[1,36,64,64]{2,1,3,0:T(8,128)S(1)} %constant_dynamic-update-slice_fusion, f32[1,36,3,64]{2,1,3,0:T(8,128)} %slice_add_fusion, s32[]{:T(128)} %constant.141.clone.1, s32[]{:T(128)} %constant.141.clone.1, s32[]{:T(128)} %constant.153.clone.1, s32[]{:T(128)} %constant.141.clone.1) | dynamic-update-slice | bytes 55300 | tf_op jit(solution)/shard_map/scatter-add | solution.py:63
  261.7 10.7 %all-gather = f32[256,64]{1,0:T(8,128)S(1)} all-gather(f32[64,64]{1,0:T(8,128)S(1)} %copy.266), channel_id=2, replica_groups=mesh['win'=4,'tile'=64] {'win'}, dimensions={0}, use_global_device_ids=true | all-gather | bytes 81920 | tf_op jit(solution)/shard_map/all_gather | solution.py:10
  (199 shorter events, 122.9 us)
Async XLA Ops:
  0.0 11.2 %copy-start = (s32[6,64]{1,0:T(8,128)S(1)}, s32[6,64]{1,0:T(8,128)}, u32[]{:S(2)}) copy-start(s32[6,64]{1,0:T(8,128)} %param.25) | copy-start | bytes 4612
  3.0 8.9 %copy-start.6 = (f32[1,36,64,64]{3,2,0,1:T(8,128)}, f32[1,36,64,64]{3,2,0,1:T(8,128)S(1)}, u32[]{:S(2)}) copy-start(f32[1,36,64,64]{3,2,0,1:T(8,128)S(1)} %reshape_squeeze.3) | copy-start | bytes 1769476
  7.3 5.3 %copy-start.22 = (bf16[1,1,36,4096]{3,2,1,0:T(8,128)(2,1)S(1)}, bf16[1,1,36,4096]{3,2,1,0:T(8,128)(2,1)}, u32[]{:S(2)}) copy-start(bf16[1,1,36,4096]{3,2,1,0:T(8,128)(2,1)} %param.18) | copy-start | bytes 884740
  7.3 9.4 %collective-permute-start = (f32[2,1,36,3,64]{4,0,3,2,1:T(2,128)S(1)}, f32[2,1,36,3,64]{4,0,3,2,1:T(2,128)S(1)}, u32[]{:S(2)}, u32[]{:S(2)}) collective-permute-start(f32[2,1,36,3,64]{4,0,3,2,1:T(2,128)S(1)} %pad_maximum_fusion.9), channel_id=1, source_target_pairs={{48,0},{49,1},{50,2},{51,3},{52,4},{53,5},{54,6},{55,7},{56,8},{57... | collective-permute-start | bytes 165896 | tf_op jit(solution)/shard_map/ppermute | solution.py:18
  9.4 12.0 %collective-permute-start.1 = (f32[2,1,36,3,64]{4,0,3,2,1:T(2,128)S(1)}, f32[2,1,36,3,64]{4,0,3,2,1:T(2,128)S(1)}, u32[]{:S(2)}, u32[]{:S(2)}) collective-permute-start(f32[2,1,36,3,64]{4,0,3,2,1:T(2,128)S(1)} %pad_maximum_fusion.9), channel_id=1, source_target_pairs={{63,0},{0,1},{1,2},{2,3},{3,4},{4,5},{5,6},{6,7},{7,8},{8,9},{9,10... | collective-permute-start | bytes 165896 | tf_op jit(solution)/shard_map/ppermute | solution.py:18
  12.6 3.5 %copy-start.28 = (f32[36]{0:T(128)S(1)}, f32[36]{0:T(128)}, u32[]{:S(2)}) copy-start(f32[36]{0:T(128)} %param.22) | copy-start | bytes 436
  40.7 2.8 %copy-start.11 = (f32[1,36,64,64]{3,1,2,0:T(8,128)S(1)}, f32[1,36,64,64]{3,1,2,0:T(8,128)}, u32[]{:S(2)}) copy-start(f32[1,36,64,64]{3,1,2,0:T(8,128)} %get-tuple-element.83) | copy-start | bytes 1769476
  45.8 20.6 %copy-start.2 = (f32[1,36,64,64]{3,1,2,0:T(8,128)}, f32[1,36,64,64]{3,1,2,0:T(8,128)S(1)}, u32[]{:S(2)}) copy-start(f32[1,36,64,64]{3,1,2,0:T(8,128)S(1)} %fusion.30) | copy-start | bytes 1769476
  47.3 5.9 %copy-start.23 = (bf16[1,1,36,4096]{3,2,1,0:T(8,128)(2,1)S(1)}, bf16[1,1,36,4096]{3,2,1,0:T(8,128)(2,1)}, u32[]{:S(2)}) copy-start(bf16[1,1,36,4096]{3,2,1,0:T(8,128)(2,1)} %param.19) | copy-start | bytes 884740
  49.1 7.3 %collective-permute-start.2 = (f32[2,1,36,3,64]{4,2,3,1,0:T(8,128)S(1)}, f32[2,1,36,3,64]{4,2,3,1,0:T(8,128)S(1)}, u32[]{:S(2)}, u32[]{:S(2)}) collective-permute-start(f32[2,1,36,3,64]{4,2,3,1,0:T(8,128)S(1)} %pad_maximum_fusion.6), channel_id=1, source_target_pairs={{32,0},{33,1},{34,2},{35,3},{36,4},{37,5},{38,6},{39,7},{40,8},{41... | collective-permute-start | bytes 165896 | tf_op jit(solution)/shard_map/ppermute | solution.py:18
  50.7 13.2 %collective-permute-start.3 = (f32[2,1,36,3,64]{4,2,3,1,0:T(8,128)S(1)}, f32[2,1,36,3,64]{4,2,3,1,0:T(8,128)S(1)}, u32[]{:S(2)}, u32[]{:S(2)}) collective-permute-start(f32[2,1,36,3,64]{4,2,3,1,0:T(8,128)S(1)} %pad_maximum_fusion.6), channel_id=1, source_target_pairs={{62,0},{63,1},{0,2},{1,3},{2,4},{3,5},{4,6},{5,7},{6,8},{7,9},{8,1... | collective-permute-start | bytes 165896 | tf_op jit(solution)/shard_map/ppermute | solution.py:18
  66.4 1.8 copy-start.3
  66.4 1.8 copy-start.24
  71.8 5.0 %collective-permute-start.4 = (f32[2,1,36,3,64]{4,2,3,1,0:T(8,128)S(1)}, f32[2,1,36,3,64]{4,2,3,1,0:T(8,128)S(1)}, u32[]{:S(2)}, u32[]{:S(2)}) collective-permute-start(f32[2,1,36,3,64]{4,2,3,1,0:T(8,128)S(1)} %pad_maximum_fusion.7), channel_id=1, source_target_pairs={{48,0},{49,1},{50,2},{51,3},{52,4},{53,5},{54,6},{55,7},{56,8},{57... | collective-permute-start | bytes 165896 | tf_op jit(solution)/shard_map/ppermute | solution.py:18
  71.9 9.5 %collective-permute-start.5 = (f32[2,1,36,3,64]{4,2,3,1,0:T(8,128)S(1)}, f32[2,1,36,3,64]{4,2,3,1,0:T(8,128)S(1)}, u32[]{:S(2)}, u32[]{:S(2)}) collective-permute-start(f32[2,1,36,3,64]{4,2,3,1,0:T(8,128)S(1)} %pad_maximum_fusion.7), channel_id=1, source_target_pairs={{63,0},{0,1},{1,2},{2,3},{3,4},{4,5},{5,6},{6,7},{7,8},{8,9},{9,10... | collective-permute-start | bytes 165896 | tf_op jit(solution)/shard_map/ppermute | solution.py:18
  98.3 2.5 copy-start.5
  100.2 5.3 %collective-permute-start.6 = (f32[2,1,36,3,64]{4,2,3,1,0:T(8,128)S(1)}, f32[2,1,36,3,64]{4,2,3,1,0:T(8,128)S(1)}, u32[]{:S(2)}, u32[]{:S(2)}) collective-permute-start(f32[2,1,36,3,64]{4,2,3,1,0:T(8,128)S(1)} %pad_maximum_fusion.8), channel_id=1, source_target_pairs={{32,0},{33,1},{34,2},{35,3},{36,4},{37,5},{38,6},{39,7},{40,8},{41... | collective-permute-start | bytes 165896 | tf_op jit(solution)/shard_map/ppermute | solution.py:18
  100.3 10.9 %collective-permute-start.7 = (f32[2,1,36,3,64]{4,2,3,1,0:T(8,128)S(1)}, f32[2,1,36,3,64]{4,2,3,1,0:T(8,128)S(1)}, u32[]{:S(2)}, u32[]{:S(2)}) collective-permute-start(f32[2,1,36,3,64]{4,2,3,1,0:T(8,128)S(1)} %pad_maximum_fusion.8), channel_id=1, source_target_pairs={{62,0},{63,1},{0,2},{1,3},{2,4},{3,5},{4,6},{5,7},{6,8},{7,9},{8,1... | collective-permute-start | bytes 165896 | tf_op jit(solution)/shard_map/ppermute | solution.py:18
  121.5 2.9 %slice-start = ((f32[1,36,64,64]{3,1,2,0:T(8,128)}), f32[1,36,63,64]{3,1,2,0:T(8,128)S(1)}, s32[]{:S(2)}) async-start(f32[1,36,64,64]{3,1,2,0:T(8,128)} %copy-done.14), calls=%async_computation | async-start | bytes 2580480 | tf_op jit(solution)/shard_map/transpose(jvp())/split | solution.py:34
  129.6 2.9 %copy-start.8 = (f32[1,36,64,64]{3,2,0,1:T(8,128)S(1)}, f32[1,36,64,64]{3,2,0,1:T(8,128)}, u32[]{:S(2)}) copy-start(f32[1,36,64,64]{3,2,0,1:T(8,128)} %reshape.558) | copy-start | bytes 1769476
  145.3 3.0 %copy-start.18 = (f32[1,36,3,64]{2,1,3,0:T(8,128)S(1)}, f32[1,36,3,64]{2,1,3,0:T(8,128)}, u32[]{:S(2)}) copy-start(f32[1,36,3,64]{2,1,3,0:T(8,128)} %rev.88) | copy-start | bytes 82948
  154.9 10.2 %collective-permute-start.9 = (f32[2,1,36,3,64]{4,0,3,2,1:T(2,128)S(1)}, f32[2,1,36,3,64]{4,0,3,2,1:T(2,128)S(1)}, u32[]{:S(2)}, u32[]{:S(2)}) collective-permute-start(f32[2,1,36,3,64]{4,0,3,2,1:T(2,128)S(1)} %copy.250), channel_id=1, source_target_pairs={{32,0},{33,1},{34,2},{35,3},{36,4},{37,5},{38,6},{39,7},{40,8},{41... | collective-permute-start | bytes 165896 | tf_op jit(solution)/shard_map/ppermute | solution.py:18
  159.6 5.5 %collective-permute-start.8 = (f32[2,1,36,3,64]{4,0,3,2,1:T(2,128)S(1)}, f32[2,1,36,3,64]{4,0,3,2,1:T(2,128)S(1)}, u32[]{:S(2)}, u32[]{:S(2)}) collective-permute-start(f32[2,1,36,3,64]{4,0,3,2,1:T(2,128)S(1)} %copy.248), channel_id=1, source_target_pairs={{2,0},{3,1},{4,2},{5,3},{6,4},{7,5},{8,6},{9,7},{10,8},{11,9},{12,... | collective-permute-start | bytes 165896 | tf_op jit(solution)/shard_map/ppermute | solution.py:18
  187.5 4.1 %copy-start.9 = (f32[1,36,64,64]{3,2,0,1:T(8,128)S(1)}, f32[1,36,64,64]{3,2,0,1:T(8,128)}, u32[]{:S(2)}) copy-start(f32[1,36,64,64]{3,2,0,1:T(8,128)} %reshape.557) | copy-start | bytes 1769476
  187.5 4.1 %copy-start.12 = (f32[1,36,64,64]{3,1,2,0:T(8,128)S(1)}, f32[1,36,64,64]{3,1,2,0:T(8,128)}, u32[]{:S(2)}) copy-start(f32[1,36,64,64]{3,1,2,0:T(8,128)} %neg.17) | copy-start | bytes 1769476
  197.6 2.6 copy-start.15
  202.3 3.7 %copy-start.16 = (f32[1,36,3,64]{2,1,3,0:T(8,128)S(1)}, f32[1,36,3,64]{2,1,3,0:T(8,128)}, u32[]{:S(2)}) copy-start(f32[1,36,3,64]{2,1,3,0:T(8,128)} %rev.92) | copy-start | bytes 82948
  202.3 3.7 %copy-start.17 = (f32[1,36,3,64]{2,1,3,0:T(8,128)S(1)}, f32[1,36,3,64]{2,1,3,0:T(8,128)}, u32[]{:S(2)}) copy-start(f32[1,36,3,64]{2,1,3,0:T(8,128)} %rev.93) | copy-start | bytes 82948
  211.4 9.4 %collective-permute-start.10 = (f32[2,1,36,3,64]{4,0,3,2,1:T(2,128)S(1)}, f32[2,1,36,3,64]{4,0,3,2,1:T(2,128)S(1)}, u32[]{:S(2)}, u32[]{:S(2)}) collective-permute-start(f32[2,1,36,3,64]{4,0,3,2,1:T(2,128)S(1)} %copy.260), channel_id=1, source_target_pairs={{1,0},{2,1},{3,2},{4,3},{5,4},{6,5},{7,6},{8,7},{9,8},{10,9},{11,1... | collective-permute-start | bytes 165896 | tf_op jit(solution)/shard_map/ppermute | solution.py:18
  214.9 2.9 %copy-start.13 = (f32[1,36,64,64]{2,1,3,0:T(8,128)S(1)}, f32[1,36,64,64]{2,1,3,0:T(8,128)}, u32[]{:S(2)}) copy-start(f32[1,36,64,64]{2,1,3,0:T(8,128)} %copy.255) | copy-start | bytes 1769476
  217.5 5.7 %collective-permute-start.11 = (f32[2,1,36,3,64]{4,0,3,2,1:T(2,128)S(1)}, f32[2,1,36,3,64]{4,0,3,2,1:T(2,128)S(1)}, u32[]{:S(2)}, u32[]{:S(2)}) collective-permute-start(f32[2,1,36,3,64]{4,0,3,2,1:T(2,128)S(1)} %copy.261), channel_id=1, source_target_pairs={{16,0},{17,1},{18,2},{19,3},{20,4},{21,5},{22,6},{23,7},{24,8},{25... | collective-permute-start | bytes 165896 | tf_op jit(solution)/shard_map/ppermute | solution.py:18
  243.0 30.0 %copy-start.1 = (s32[6,64]{1,0:T(8,128)S(1)}, s32[6,64]{1,0:T(8,128)}, u32[]{:S(2)}) copy-start(s32[6,64]{1,0:T(8,128)} %param.25) | copy-start | bytes 4612
  (10 other events, 12.2 us)
